TPU v7x, 512 devices: a whole 4x4x16 slice. The times are simulated.
512 devices in a mesh: row: 8 (over z_lo), col: 16 (over x, y), layer: 4 (over z_hi, core).
Axes of the slice: x: 4, y: 4, z: 16 (z_hi: 2, z_lo: 8; z = z_hi * 8 + z_lo), core: 2. Of those that a mesh axis runs over, the one named last changes fastest.
Arguments:
- doubles_amplitude_tensor: float32 [2304, 2048], P('col', 'layer'), may hold values from -6 to 6
- integrals: float32 [8, 16, 4, 96, 2048], P('row', 'col', 'layer'), may hold values from -0.125 to 0.125
- incoming_residual: float32 [2304, 49152], P('col', ('row', 'layer')), may hold values from -6 to 6
Outputs:
- updated_residual: float32 [2304, 49152], P('col', ('row', 'layer'))
All inputs are finite; a program needn't handle non-finite values.
Results may differ from a plain program's by a relative error of at most 0.00005.
Values sent between devices are 32-bit elements; how exact they have to be, the bound alone decides.
No kernel may reach another device: no remote copies, remote signals or barrier semaphores. Data moves between devices by JAX's collectives and lax.ppermute only.
A program may use at most 64 MiB of HBM per device.

v0:
```python
import jax
import jax.numpy as jnp
from jax import lax
from jax.sharding import PartitionSpec as P


def regroup(integrals):
    local = integrals.reshape(1, integrals.shape[3], integrals.shape[4])
    return lax.all_to_all(local, "layer", split_axis=2, concat_axis=0, tiled=True)


def on_device(doubles_amplitude_tensor, integrals, incoming_residual):
    ij_rows = doubles_amplitude_tensor.shape[0]
    regrouped = regroup(integrals)[None]
    partial_ladder_value = jnp.einsum(
        "ic,nlkc->inlk",
        doubles_amplitude_tensor,
        lax.all_gather(regrouped, "col", axis=0, tiled=True),
        precision=lax.Precision.HIGHEST,
        preferred_element_type=jnp.float32,
    )
    summed = lax.psum_scatter(partial_ladder_value, "layer", scatter_dimension=2, tiled=True)
    return incoming_residual + summed.reshape(ij_rows, -1)


def solution(mesh):
    return jax.shard_map(
        on_device,
        mesh=mesh,
        in_specs=(
            P("col", "layer"),
            P("row", "col", "layer", None, None),
            P("col", ("row", "layer")),
        ),
        out_specs=P("col", ("row", "layer")),
        check_vma=False,
    )
```

profile of v0, /device:TPU:1, one launch (start us, length us, event | category | flops | bytes accessed | tf_op | source)
XLA Modules:
  0.0 565.8 jit_solution(12398285052435293716)
XLA Ops:
  6.5 0.0 copy-start
  6.5 0.0 all-gather.3.cloned.1.call-start
  6.5 1.5 copy.7
  8.1 43.3 %all_to_all.15 = f32[1,96,2048]{1,0,2:T(1,128)S(1)} all-to-all(f32[1,96,2048]{1,0,2:T(1,128)S(1)} %bitcast.24), channel_id=1, replica_groups=mesh['row'=8,'col'=16,'layer'=4] {'layer'}, dimensions={2} | all-to-all | bytes 1572864 | tf_op jit(solution)/shard_map/all_to_all | solution.py:9
  51.4 1.2 copy.8
  52.6 0.0 all-gather.3.cloned.1.call-update
  52.6 0.0 all-reduce.3.cloned.1.call-start
  52.6 128.7 %all-gather.3.cloned.1.call-done = f32[64,1,96,512]{3,2,1,0:T(8,128)} async-done(((f32[4,1,96,512]{3,2,1,0:T(8,128)}), f32[64,1,96,512]{3,2,1,0:T(8,128)}) %all-gather.3.cloned.1.call-update) | async-done | bytes 12582928 | tf_op jit(solution)/shard_map/all_gather | solution.py:18
  181.3 0.0 copy-done
  181.4 18.7 %fusion = f32[144,16,4,96]{3,0,2,1:T(8,128)} fusion(f32[144,512]{1,0:T(8,128)S(1)} %copy-done, f32[16,4,96,512]{3,2,1,0:T(8,128)} %bitcast.22), kind=kOutput, calls=%fused_computation | convolution fusion | flops 5435817984 | bytes 16416768 | tf_op jit(solution)/shard_map/ic,nlkc->inlk/dot_general | solution.py:15
  200.1 0.0 copy-start.1
  200.1 0.0 all-reduce.3.cloned.1.call-update
  200.1 1.3 dynamic-slice
  201.5 353.6 %all-reduce.3.cloned.1.call-done = f32[144,16,4,96]{3,0,2,1:T(8,128)} async-done(((f32[144,16,4,96]{3,0,2,1:T(8,128)}), f32[144,16,4,96]{3,0,2,1:T(8,128)}) %all-reduce.3.cloned.1.call-update) | async-done | bytes 3538960
  555.1 2.0 constant_dynamic-slice_fusion
  557.1 0.4 copy.9
  557.5 0.5 reshape.8
  558.0 0.0 copy-done.1
  558.0 1.0 add.5
Async XLA Ops:
  6.5 174.8 %copy-start = (f32[144,512]{1,0:T(8,128)S(1)}, f32[144,512]{1,0:T(8,128)}, u32[]{:S(2)}) copy-start(f32[144,512]{1,0:T(8,128)} %param.3) | copy-start | bytes 884740
  6.5 174.8 %all-gather.3.cloned.1.call-start = ((), (), s32[]{:S(2)}) async-start(), calls=%async_computation.1 | async-start | bytes 13369344 | tf_op jit(solution)/shard_map/all_gather | solution.py:18
  52.6 502.5 %all-reduce.3.cloned.1.call-start = ((), (), s32[]{:S(2)}) async-start(), calls=%async_computation.2 | async-start | bytes 9437184
  200.1 357.9 %copy-start.1 = (f32[144,1536]{1,0:T(8,128)S(1)}, f32[144,1536]{1,0:T(8,128)}, u32[]{:S(2)}) copy-start(f32[144,1536]{1,0:T(8,128)} %param.5) | copy-start | bytes 2654212
Sparse Core Ops, SparseCore 0:
  52.7 128.5 all-gather.2
  200.2 354.7 all-reduce.2
where the time goes:
time: 566 us
  waiting for transfers between devices  482 us (85%)
  blocking collectives  43.3 us (8%)
  matrix products  18.7 us (3%)
  between operations  13.4 us (2%)
  local copies, waits for them, and re-layouts  6.95 us (1%)
    unnamed x3, waiting for transfers between devices  354 us
    all_gather x1, waiting for transfers between devices, on_device(): lax.all_gather(regrouped, 'col', axis=0, tiled=True)  129 us
    all_to_all x1, blocking collectives, regroup(): lax.all_to_all(local, 'layer', split_axis=2, concat_axis=0, tiled=True)  43.3 us
    dot_general x1, matrix products, on_device(): jnp.einsum('ic,nlkc->inlk', doubles_amplitude_tensor, lax.all_gather(regr...  18.7 us
  transfers between devices with their start and end apart: 2, of which 2 were waited for; matrix products, arithmetic and copies ran while one was open for 0% of the time, Pallas kernels for 0%

commit v1 on v0

--- a/solution.py
+++ b/solution.py
@@ -2,6 +2,28 @@
 import jax.numpy as jnp
 from jax import lax
 from jax.sharding import PartitionSpec as P
+
+
+def in_order(parts, dim):
+    parts = jnp.moveaxis(parts, 0, dim)
+    shape = parts.shape
+    return parts.reshape(*shape[:dim], shape[dim] * shape[dim + 1], *shape[dim + 2 :])
+
+
+def gather_around(x, axis, dim):
+    size = lax.axis_size(axis)
+    pairs = [(i, (i + 1) % size) for i in range(size)]
+    back = [(b, a) for a, b in pairs]
+    lower, upper = ([], [])
+    for step in range(size - 1):
+        if step % 2 == 0:
+            lower.append(lax.ppermute(lower[-1] if lower else x, axis, pairs))
+        else:
+            upper.append(lax.ppermute(upper[-1] if upper else x, axis, back))
+    pieces = jnp.stack([*lower[::-1], x, *upper])
+    shift = lax.axis_index(axis) - len(lower)
+    pieces = pieces[(jnp.arange(size) - shift) % size]
+    return in_order(pieces, dim)
 
 
 def regroup(integrals):
@@ -15,7 +37,7 @@
     partial_ladder_value = jnp.einsum(
         "ic,nlkc->inlk",
         doubles_amplitude_tensor,
-        lax.all_gather(regrouped, "col", axis=0, tiled=True),
+        gather_around(regrouped, "col", 0),
         precision=lax.Precision.HIGHEST,
         preferred_element_type=jnp.float32,
     )

time: 566 us -> 662 us (1.17)
  starting transfers between devices: 0.04 us -> 65.9 us
  local copies, waits for them, and re-layouts: 6.95 us -> 44.5 us
  waiting for transfers between devices: 482 us -> 473 us
    all_gather x1 -> x0, waiting for transfers between devices: 129 us -> none  [on_device(): lax.all_gather(regrouped, 'col', axis=0, tiled=True)]
    ppermute x0 -> x15, waiting for transfers between devices: none -> 93.3 us  [the longest x8 92.1 us: gather_around(): lower.append(lax.ppermute(lower[-1] if lower else x, axis, pairs))]
    ppermute x0 -> x15, starting transfers between devices: none -> 65.9 us  [the longest x7 49.3 us: gather_around(): upper.append(lax.ppermute(upper[-1] if upper else x, axis, back))]
    unnamed x7 -> x38, local copies, waits for them, and re-layouts: 4.85 us -> 31.9 us
    unnamed x3 -> x2, waiting for transfers between devices: 354 us -> 380 us
    gather x0 -> x1, local copies, waits for them, and re-layouts: none -> 10.4 us  [gather_around(): pieces = pieces[(jnp.arange(size) - shift) % size]]
  transfers between devices with their start and end apart: 2 -> 16, of which waited for: 2 -> 11; matrix products, arithmetic and copies ran while one was open for 0% -> 4% of each run, Pallas kernels for 0% -> 0%
where the time goes in v1:
time: 662 us; the launch traced here: 661 us
  waiting for transfers between devices  473 us (71%)
  starting transfers between devices  65.9 us (10%)
  local copies, waits for them, and re-layouts  44.5 us (7%)
  blocking collectives  43.3 us (7%)
  matrix products  19.3 us (3%)
  between operations  13.7 us (2%)
    unnamed x2, waiting for transfers between devices  380 us
    ppermute x8, waiting for transfers between devices, gather_around(): lower.append(lax.ppermute(lower[-1] if lower else x, axis, pairs))  92.1 us
    ppermute x7, starting transfers between devices, gather_around(): upper.append(lax.ppermute(upper[-1] if upper else x, axis, back))  49.3 us
    all_to_all x1, blocking collectives, regroup(): lax.all_to_all(local, 'layer', split_axis=2, concat_axis=0, tiled=True)  43.3 us
    unnamed x38, local copies, waits for them, and re-layouts  31.9 us
    dot_general x1, matrix products, on_device(): jnp.einsum('ic,nlkc->inlk', doubles_amplitude_tensor, gather_around(regro...  19.3 us
    ppermute x8, starting transfers between devices, gather_around(): lower.append(lax.ppermute(lower[-1] if lower else x, axis, pairs))  16.6 us
  transfers between devices with their start and end apart: 16, of which 11 were waited for; matrix products, arithmetic and copies ran while one was open for 4% of the time, Pallas kernels for 0%

profile of v1, /device:TPU:1, one launch (start us, length us, event | category | flops | bytes accessed | tf_op | source)
XLA Modules:
  0.0 661.2 jit_solution(11391801111458867324)
XLA Ops:
  8.1 43.3 %all_to_all.15 = f32[1,96,2048]{1,0,2:T(1,128)S(1)} all-to-all(f32[1,96,2048]{1,0,2:T(1,128)S(1)} %bitcast.89), channel_id=1, replica_groups=mesh['row'=8,'col'=16,'layer'=4] {'layer'}, dimensions={2} | all-to-all | bytes 1572864 | tf_op jit(solution)/shard_map/all_to_all | solution.py:31
  51.7 3.2 collective-permute-start
  54.9 20.3 %collective-permute-done = f32[1,4,96,512]{3,2,1,0:T(8,128)S(1)} collective-permute-done((f32[1,4,96,512]{3,2,1,0:T(8,128)S(1)}, f32[1,4,96,512]{3,2,1,0:T(8,128)S(1)}, u32[]{:S(2)}, u32[]{:S(2)}) %collective-permute-start) | collective-permute-done | bytes 786464 | tf_op jit(solution)/shard_map/ppermute | solution.py:20
  77.1 6.7 %collective-permute-start.8 = (f32[1,4,96,512]{3,2,1,0:T(8,128)S(1)}, f32[1,4,96,512]{3,2,1,0:T(8,128)S(1)}, u32[]{:S(2)}, u32[]{:S(2)}) collective-permute-start(f32[1,4,96,512]{3,2,1,0:T(8,128)S(1)} %bitcast.91), channel_id=1, source_target_pairs={{4,0},{8,4},{12,8},{16,12},{20,16},{24,20},{28,24},{32,28},{36,32}... | collective-permute-start | bytes 2359304 | tf_op jit(solution)/shard_map/ppermute | solution.py:22
  83.8 13.9 %collective-permute-done.1 = f32[1,4,96,512]{3,2,1,0:T(8,128)} collective-permute-done((f32[1,4,96,512]{3,2,1,0:T(8,128)S(1)}, f32[1,4,96,512]{3,2,1,0:T(8,128)}, u32[]{:S(2)}, u32[]{:S(2)}) %collective-permute-start.1) | collective-permute-done | bytes 786464 | tf_op jit(solution)/shard_map/ppermute | solution.py:20
  99.6 6.7 %collective-permute-start.9 = (f32[1,4,96,512]{3,2,1,0:T(8,128)S(1)}, f32[1,4,96,512]{3,2,1,0:T(8,128)S(1)}, u32[]{:S(2)}, u32[]{:S(2)}) collective-permute-start(f32[1,4,96,512]{3,2,1,0:T(8,128)S(1)} %collective-permute-done.8), channel_id=1, source_target_pairs={{4,0},{8,4},{12,8},{16,12},{20,16},{24,20},{28,24},{32,28},{36,32}... | collective-permute-start | bytes 2359304 | tf_op jit(solution)/shard_map/ppermute | solution.py:22
  106.3 13.2 %collective-permute-done.2 = f32[1,4,96,512]{3,2,1,0:T(8,128)} collective-permute-done((f32[1,4,96,512]{3,2,1,0:T(8,128)}, f32[1,4,96,512]{3,2,1,0:T(8,128)}, u32[]{:S(2)}, u32[]{:S(2)}) %collective-permute-start.2) | collective-permute-done | bytes 786464 | tf_op jit(solution)/shard_map/ppermute | solution.py:20
  122.2 6.7 %collective-permute-start.10 = (f32[1,4,96,512]{3,2,1,0:T(8,128)S(1)}, f32[1,4,96,512]{3,2,1,0:T(8,128)S(1)}, u32[]{:S(2)}, u32[]{:S(2)}) collective-permute-start(f32[1,4,96,512]{3,2,1,0:T(8,128)S(1)} %collective-permute-done.9), channel_id=1, source_target_pairs={{4,0},{8,4},{12,8},{16,12},{20,16},{24,20},{28,24},{32,28},{36,32}... | collective-permute-start | bytes 2359304 | tf_op jit(solution)/shard_map/ppermute | solution.py:22
  128.9 11.3 %collective-permute-done.3 = f32[1,4,96,512]{3,2,1,0:T(8,128)} collective-permute-done((f32[1,4,96,512]{3,2,1,0:T(8,128)}, f32[1,4,96,512]{3,2,1,0:T(8,128)}, u32[]{:S(2)}, u32[]{:S(2)}) %collective-permute-start.3) | collective-permute-done | bytes 786464 | tf_op jit(solution)/shard_map/ppermute | solution.py:20
  143.1 7.0 %collective-permute-start.11 = (f32[1,4,96,512]{3,2,1,0:T(8,128)S(1)}, f32[1,4,96,512]{3,2,1,0:T(8,128)S(1)}, u32[]{:S(2)}, u32[]{:S(2)}) collective-permute-start(f32[1,4,96,512]{3,2,1,0:T(8,128)S(1)} %collective-permute-done.10), channel_id=1, source_target_pairs={{4,0},{8,4},{12,8},{16,12},{20,16},{24,20},{28,24},{32,28},{36,32}... | collective-permute-start | bytes 2359304 | tf_op jit(solution)/shard_map/ppermute | solution.py:22
  150.1 10.0 %collective-permute-done.4 = f32[1,4,96,512]{3,2,1,0:T(8,128)S(1)} collective-permute-done((f32[1,4,96,512]{3,2,1,0:T(8,128)}, f32[1,4,96,512]{3,2,1,0:T(8,128)S(1)}, u32[]{:S(2)}, u32[]{:S(2)}) %collective-permute-start.4) | collective-permute-done | bytes 786464 | tf_op jit(solution)/shard_map/ppermute | solution.py:20
  162.9 7.4 %collective-permute-start.12 = (f32[1,4,96,512]{3,2,1,0:T(8,128)S(1)}, f32[1,4,96,512]{3,2,1,0:T(8,128)}, u32[]{:S(2)}, u32[]{:S(2)}) collective-permute-start(f32[1,4,96,512]{3,2,1,0:T(8,128)S(1)} %collective-permute-done.11), channel_id=1, source_target_pairs={{4,0},{8,4},{12,8},{16,12},{20,16},{24,20},{28,24},{32,28},{36,32}... | collective-permute-start | bytes 2359304 | tf_op jit(solution)/shard_map/ppermute | solution.py:22
  170.3 8.5 %collective-permute-done.5 = f32[1,4,96,512]{3,2,1,0:T(8,128)S(1)} collective-permute-done((f32[1,4,96,512]{3,2,1,0:T(8,128)S(1)}, f32[1,4,96,512]{3,2,1,0:T(8,128)S(1)}, u32[]{:S(2)}, u32[]{:S(2)}) %collective-permute-start.5) | collective-permute-done | bytes 786464 | tf_op jit(solution)/shard_map/ppermute | solution.py:20
  181.3 7.5 %collective-permute-start.13 = (f32[1,4,96,512]{3,2,1,0:T(8,128)}, f32[1,4,96,512]{3,2,1,0:T(8,128)}, u32[]{:S(2)}, u32[]{:S(2)}) collective-permute-start(f32[1,4,96,512]{3,2,1,0:T(8,128)} %collective-permute-done.12), channel_id=1, source_target_pairs={{4,0},{8,4},{12,8},{16,12},{20,16},{24,20},{28,24},{32,28},{36,32}... | collective-permute-start | bytes 2359304 | tf_op jit(solution)/shard_map/ppermute | solution.py:22
  188.8 7.8 %collective-permute-done.6 = f32[1,4,96,512]{3,2,1,0:T(8,128)} collective-permute-done((f32[1,4,96,512]{3,2,1,0:T(8,128)S(1)}, f32[1,4,96,512]{3,2,1,0:T(8,128)}, u32[]{:S(2)}, u32[]{:S(2)}) %collective-permute-start.6) | collective-permute-done | bytes 786464 | tf_op jit(solution)/shard_map/ppermute | solution.py:20
  199.2 7.4 %collective-permute-start.14 = (f32[1,4,96,512]{3,2,1,0:T(8,128)}, f32[1,4,96,512]{3,2,1,0:T(8,128)S(1)}, u32[]{:S(2)}, u32[]{:S(2)}) collective-permute-start(f32[1,4,96,512]{3,2,1,0:T(8,128)} %collective-permute-done.13), channel_id=1, source_target_pairs={{4,0},{8,4},{12,8},{16,12},{20,16},{24,20},{28,24},{32,28},{36,32}... | collective-permute-start | bytes 2359304 | tf_op jit(solution)/shard_map/ppermute | solution.py:22
  206.6 7.2 %collective-permute-done.7 = f32[1,4,96,512]{3,2,1,0:T(8,128)} collective-permute-done((f32[1,4,96,512]{3,2,1,0:T(8,128)}, f32[1,4,96,512]{3,2,1,0:T(8,128)}, u32[]{:S(2)}, u32[]{:S(2)}) %collective-permute-start.7) | collective-permute-done | bytes 786464 | tf_op jit(solution)/shard_map/ppermute | solution.py:20
  215.9 2.1 bitcast_dynamic-update-slice_fusion.13
  220.1 2.1 bitcast_dynamic-update-slice_fusion.11
  222.1 2.1 bitcast_dynamic-update-slice_fusion.10
  226.3 2.1 bitcast_dynamic-update-slice_fusion.8
  239.2 10.4 %gather_fusion = f32[16,4,96,512]{3,2,1,0:T(8,128)} fusion(f32[16,4,96,512]{3,2,1,0:T(8,128)} %bitcast.36, s32[1024]{0:T(1024)S(1)} %pad_clamp_fusion), kind=kCustom, calls=%fused_computation | custom fusion | bytes 25165888 | tf_op jit(solution)/shard_map/gather | solution.py:25
  249.6 19.3 %convolution_bitcast_fusion = f32[144,16,4,96]{3,0,2,1:T(8,128)} fusion(f32[16,4,96,512]{3,2,1,0:T(8,128)} %gather_fusion, f32[144,512]{1,0:T(8,128)S(1)} %copy-done), kind=kOutput, calls=%fused_computation.1 | convolution fusion | flops 5435817984 | bytes 16416768 | tf_op jit(solution)/shard_map/ic,nlkc->inlk/dot_general | solution.py:37
  270.3 380.2 %all-reduce.3.cloned.1.call-done = f32[144,16,4,96]{3,0,2,1:T(8,128)} async-done(((f32[144,16,4,96]{3,0,2,1:T(8,128)}), f32[144,16,4,96]{3,0,2,1:T(8,128)}) %all-reduce.3.cloned.1.call-update) | async-done | bytes 3538960
  (57 shorter events, 41.3 us)
Async XLA Ops:
  6.5 243.1 %copy-start = (f32[144,512]{1,0:T(8,128)S(1)}, f32[144,512]{1,0:T(8,128)}, u32[]{:S(2)}) copy-start(f32[144,512]{1,0:T(8,128)} %param.3) | copy-start | bytes 884740
  6.5 643.9 %all-reduce.3.cloned.1.call-start = ((), (), s32[]{:S(2)}) async-start(), calls=%async_computation.1 | async-start | bytes 9437184
  51.7 23.5 %collective-permute-start = (f32[1,4,96,512]{3,2,1,0:T(8,128)S(1)}, f32[1,4,96,512]{3,2,1,0:T(8,128)S(1)}, u32[]{:S(2)}, u32[]{:S(2)}) collective-permute-start(f32[1,4,96,512]{3,2,1,0:T(8,128)S(1)} %bitcast.90), channel_id=1, source_target_pairs={{0,4},{4,8},{8,12},{12,16},{16,20},{20,24},{24,28},{28,32},{32,36}... | collective-permute-start | bytes 2359304 | tf_op jit(solution)/shard_map/ppermute | solution.py:20
  75.2 22.5 %collective-permute-start.1 = (f32[1,4,96,512]{3,2,1,0:T(8,128)S(1)}, f32[1,4,96,512]{3,2,1,0:T(8,128)}, u32[]{:S(2)}, u32[]{:S(2)}) collective-permute-start(f32[1,4,96,512]{3,2,1,0:T(8,128)S(1)} %collective-permute-done), channel_id=1, source_target_pairs={{0,4},{4,8},{8,12},{12,16},{16,20},{20,24},{24,28},{28,32},{32,36}... | collective-permute-start | bytes 2359304 | tf_op jit(solution)/shard_map/ppermute | solution.py:20
  77.1 22.5 %collective-permute-start.8 = (f32[1,4,96,512]{3,2,1,0:T(8,128)S(1)}, f32[1,4,96,512]{3,2,1,0:T(8,128)S(1)}, u32[]{:S(2)}, u32[]{:S(2)}) collective-permute-start(f32[1,4,96,512]{3,2,1,0:T(8,128)S(1)} %bitcast.91), channel_id=1, source_target_pairs={{4,0},{8,4},{12,8},{16,12},{20,16},{24,20},{28,24},{32,28},{36,32}... | collective-permute-start | bytes 2359304 | tf_op jit(solution)/shard_map/ppermute | solution.py:22
  97.6 21.8 %collective-permute-start.2 = (f32[1,4,96,512]{3,2,1,0:T(8,128)}, f32[1,4,96,512]{3,2,1,0:T(8,128)}, u32[]{:S(2)}, u32[]{:S(2)}) collective-permute-start(f32[1,4,96,512]{3,2,1,0:T(8,128)} %collective-permute-done.1), channel_id=1, source_target_pairs={{0,4},{4,8},{8,12},{12,16},{16,20},{20,24},{24,28},{28,32},{32,36}... | collective-permute-start | bytes 2359304 | tf_op jit(solution)/shard_map/ppermute | solution.py:20
  99.6 21.8 %collective-permute-start.9 = (f32[1,4,96,512]{3,2,1,0:T(8,128)S(1)}, f32[1,4,96,512]{3,2,1,0:T(8,128)S(1)}, u32[]{:S(2)}, u32[]{:S(2)}) collective-permute-start(f32[1,4,96,512]{3,2,1,0:T(8,128)S(1)} %collective-permute-done.8), channel_id=1, source_target_pairs={{4,0},{8,4},{12,8},{16,12},{20,16},{24,20},{28,24},{32,28},{36,32}... | collective-permute-start | bytes 2359304 | tf_op jit(solution)/shard_map/ppermute | solution.py:22
  119.4 20.9 %collective-permute-start.3 = (f32[1,4,96,512]{3,2,1,0:T(8,128)}, f32[1,4,96,512]{3,2,1,0:T(8,128)}, u32[]{:S(2)}, u32[]{:S(2)}) collective-permute-start(f32[1,4,96,512]{3,2,1,0:T(8,128)} %collective-permute-done.2), channel_id=1, source_target_pairs={{0,4},{4,8},{8,12},{12,16},{16,20},{20,24},{24,28},{28,32},{32,36}... | collective-permute-start | bytes 2359304 | tf_op jit(solution)/shard_map/ppermute | solution.py:20
  122.2 19.9 %collective-permute-start.10 = (f32[1,4,96,512]{3,2,1,0:T(8,128)S(1)}, f32[1,4,96,512]{3,2,1,0:T(8,128)S(1)}, u32[]{:S(2)}, u32[]{:S(2)}) collective-permute-start(f32[1,4,96,512]{3,2,1,0:T(8,128)S(1)} %collective-permute-done.9), channel_id=1, source_target_pairs={{4,0},{8,4},{12,8},{16,12},{20,16},{24,20},{28,24},{32,28},{36,32}... | collective-permute-start | bytes 2359304 | tf_op jit(solution)/shard_map/ppermute | solution.py:22
  140.3 19.8 %collective-permute-start.4 = (f32[1,4,96,512]{3,2,1,0:T(8,128)}, f32[1,4,96,512]{3,2,1,0:T(8,128)S(1)}, u32[]{:S(2)}, u32[]{:S(2)}) collective-permute-start(f32[1,4,96,512]{3,2,1,0:T(8,128)} %collective-permute-done.3), channel_id=1, source_target_pairs={{0,4},{4,8},{8,12},{12,16},{16,20},{20,24},{24,28},{28,32},{32,36}... | collective-permute-start | bytes 2359304 | tf_op jit(solution)/shard_map/ppermute | solution.py:20
  142.2 0.9 copy-start.4
  143.1 18.9 %collective-permute-start.11 = (f32[1,4,96,512]{3,2,1,0:T(8,128)S(1)}, f32[1,4,96,512]{3,2,1,0:T(8,128)S(1)}, u32[]{:S(2)}, u32[]{:S(2)}) collective-permute-start(f32[1,4,96,512]{3,2,1,0:T(8,128)S(1)} %collective-permute-done.10), channel_id=1, source_target_pairs={{4,0},{8,4},{12,8},{16,12},{20,16},{24,20},{28,24},{32,28},{36,32}... | collective-permute-start | bytes 2359304 | tf_op jit(solution)/shard_map/ppermute | solution.py:22
  160.1 21.2 %copy-start.8 = (f32[1,4,96,512]{3,2,1,0:T(8,128)}, f32[1,4,96,512]{3,2,1,0:T(8,128)S(1)}, u32[]{:S(2)}) copy-start(f32[1,4,96,512]{3,2,1,0:T(8,128)S(1)} %collective-permute-done.4) | copy-start | bytes 2359300
  160.1 18.7 %collective-permute-start.5 = (f32[1,4,96,512]{3,2,1,0:T(8,128)S(1)}, f32[1,4,96,512]{3,2,1,0:T(8,128)S(1)}, u32[]{:S(2)}, u32[]{:S(2)}) collective-permute-start(f32[1,4,96,512]{3,2,1,0:T(8,128)S(1)} %collective-permute-done.4), channel_id=1, source_target_pairs={{0,4},{4,8},{8,12},{12,16},{16,20},{20,24},{24,28},{28,32},{32,36}... | collective-permute-start | bytes 2359304 | tf_op jit(solution)/shard_map/ppermute | solution.py:20
  162.9 18.4 %collective-permute-start.12 = (f32[1,4,96,512]{3,2,1,0:T(8,128)S(1)}, f32[1,4,96,512]{3,2,1,0:T(8,128)}, u32[]{:S(2)}, u32[]{:S(2)}) collective-permute-start(f32[1,4,96,512]{3,2,1,0:T(8,128)S(1)} %collective-permute-done.11), channel_id=1, source_target_pairs={{4,0},{8,4},{12,8},{16,12},{20,16},{24,20},{28,24},{32,28},{36,32}... | collective-permute-start | bytes 2359304 | tf_op jit(solution)/shard_map/ppermute | solution.py:22
  178.8 10.1 %copy-start.9 = (f32[1,4,96,512]{3,2,1,0:T(8,128)}, f32[1,4,96,512]{3,2,1,0:T(8,128)S(1)}, u32[]{:S(2)}) copy-start(f32[1,4,96,512]{3,2,1,0:T(8,128)S(1)} %collective-permute-done.5) | copy-start | bytes 2359300
  178.8 17.9 %collective-permute-start.6 = (f32[1,4,96,512]{3,2,1,0:T(8,128)S(1)}, f32[1,4,96,512]{3,2,1,0:T(8,128)}, u32[]{:S(2)}, u32[]{:S(2)}) collective-permute-start(f32[1,4,96,512]{3,2,1,0:T(8,128)S(1)} %collective-permute-done.5), channel_id=1, source_target_pairs={{0,4},{4,8},{8,12},{12,16},{16,20},{20,24},{24,28},{28,32},{32,36}... | collective-permute-start | bytes 2359304 | tf_op jit(solution)/shard_map/ppermute | solution.py:20
  181.3 17.9 %collective-permute-start.13 = (f32[1,4,96,512]{3,2,1,0:T(8,128)}, f32[1,4,96,512]{3,2,1,0:T(8,128)}, u32[]{:S(2)}, u32[]{:S(2)}) collective-permute-start(f32[1,4,96,512]{3,2,1,0:T(8,128)} %collective-permute-done.12), channel_id=1, source_target_pairs={{4,0},{8,4},{12,8},{16,12},{20,16},{24,20},{28,24},{32,28},{36,32}... | collective-permute-start | bytes 2359304 | tf_op jit(solution)/shard_map/ppermute | solution.py:22
  196.7 17.2 %collective-permute-start.7 = (f32[1,4,96,512]{3,2,1,0:T(8,128)}, f32[1,4,96,512]{3,2,1,0:T(8,128)}, u32[]{:S(2)}, u32[]{:S(2)}) collective-permute-start(f32[1,4,96,512]{3,2,1,0:T(8,128)} %collective-permute-done.6), channel_id=1, source_target_pairs={{0,4},{4,8},{8,12},{12,16},{16,20},{20,24},{24,28},{28,32},{32,36}... | collective-permute-start | bytes 2359304 | tf_op jit(solution)/shard_map/ppermute | solution.py:20
  198.6 32.6 %copy-start.3 = (f32[1,4,96,512]{3,2,1,0:T(8,128)S(1)}, f32[1,4,96,512]{3,2,1,0:T(8,128)}, u32[]{:S(2)}) copy-start(f32[1,4,96,512]{3,2,1,0:T(8,128)} %copy-done.2) | copy-start | bytes 2359300
  198.6 33.6 %copy-start.5 = (f32[1,4,96,512]{3,2,1,0:T(8,128)S(1)}, f32[1,4,96,512]{3,2,1,0:T(8,128)}, u32[]{:S(2)}) copy-start(f32[1,4,96,512]{3,2,1,0:T(8,128)} %copy-done.4) | copy-start | bytes 2359300
  198.6 34.6 %copy-start.7 = (f32[1,4,96,512]{3,2,1,0:T(8,128)S(1)}, f32[1,4,96,512]{3,2,1,0:T(8,128)}, u32[]{:S(2)}) copy-start(f32[1,4,96,512]{3,2,1,0:T(8,128)} %copy-done.6) | copy-start | bytes 2359300
  199.2 39.0 %collective-permute-start.14 = (f32[1,4,96,512]{3,2,1,0:T(8,128)}, f32[1,4,96,512]{3,2,1,0:T(8,128)S(1)}, u32[]{:S(2)}, u32[]{:S(2)}) collective-permute-start(f32[1,4,96,512]{3,2,1,0:T(8,128)} %collective-permute-done.13), channel_id=1, source_target_pairs={{4,0},{8,4},{12,8},{16,12},{20,16},{24,20},{28,24},{32,28},{36,32}... | collective-permute-start | bytes 2359304 | tf_op jit(solution)/shard_map/ppermute | solution.py:22
  249.6 403.7 %copy-start.1 = (f32[144,1536]{1,0:T(8,128)S(1)}, f32[144,1536]{1,0:T(8,128)}, u32[]{:S(2)}) copy-start(f32[144,1536]{1,0:T(8,128)} %param.5) | copy-start | bytes 2654212
  (2 other events, 1.8 us)
Sparse Core Ops, SparseCore 0:
  269.1 381.2 all-reduce.2
